TPU v7x, 512 devices: a whole 4x4x16 slice. The times are simulated.
512 devices in a mesh: lag: 64 (over y, z_hi, x, core), col: 8 (over z_lo).
Axes of the slice: x: 4, y: 4, z: 16 (z_hi: 2, z_lo: 8; z = z_hi * 8 + z_lo), core: 2. Of those that a mesh axis runs over, the one named last changes fastest.
Arguments:
- tap_matrices: bfloat16 [64, 1024, 8192], P('lag', None, 'col'), may hold values from -0.0625 to 0.0625
- density_history: bfloat16 [256, 8192, 128], P('lag', 'col'), may hold values from -6 to 6
- offsets: int32 [64], P('lag'), may hold values from 0 to 3
- column_slots: int32 [8, 128], P('col'), may hold values from 0 to 127, each once within a row
Outputs:
- history_sum: float32 [64, 1024, 3, 128], P('lag', 'col')
Inputs may be any that keep to these rules, and one draw needn't show every extreme that they name: Section s reads history slots s * 4 + offsets[s] to s * 4 + offsets[s] + 2. `column_slots`: each row is a permutation of the 128 stored columns.
All inputs are finite; a program needn't handle non-finite values.
Results may differ from a plain program's by a relative error of at most 0.0003.
Values may be sent and summed in bfloat16 or wider, within the bound.
A program may use at most 128 MiB of HBM per device.

v0:
```python
import jax
import jax.numpy as jnp
from jax import lax
from jax.sharding import PartitionSpec as P

TICKS = 3


def shifted(value, axis, steps):
    count = lax.axis_size(axis)
    initial, last = (max(0, -steps), min(count, count - steps))
    return lax.ppermute(value, axis, [(source, source + steps) for source in range(initial, last)])


def carried_in(part, axis, combine, identity):
    place = lax.axis_index(axis)
    gathered = lax.all_gather(part, axis)
    state = jnp.zeros_like(part) + jnp.asarray(identity, part.dtype)

    def one(step, state):
        return combine(state, lax.dynamic_index_in_dim(gathered, step, 0, False))

    return lax.fori_loop(0, place, one, state)


def combine_sum(earlier, current):
    return earlier + current


def local(tap_matrices, density_history, offsets, column_slots):
    tap_matrix = tap_matrices[0]
    ordered = jnp.take(density_history, column_slots[0], axis=2)
    newer_block = shifted(ordered, "lag", -1)
    window = jnp.concatenate([ordered, newer_block], axis=0)
    densities = lax.dynamic_slice_in_dim(window, offsets[0], TICKS, 0)
    reduced = lax.psum_scatter(
        jnp.einsum("mc,tce->mte", tap_matrix, densities, preferred_element_type=jnp.float32),
        "col",
        scatter_dimension=0,
        tiled=True,
    )
    earlier = carried_in(reduced, "lag", combine_sum, jnp.zeros_like(reduced))
    history_sum = earlier + reduced
    return history_sum[None]


def solution(mesh):
    return jax.shard_map(
        local,
        mesh=mesh,
        in_specs=(P("lag", None, "col"), P("lag", "col", None), P("lag"), P("col", None)),
        out_specs=P("lag", "col", None, None),
        check_vma=False,
    )
```

profile of v0, /device:TPU:479, one launch (start us, length us, event | category | flops | bytes accessed | tf_op | source)
XLA Modules:
  0.0 488.4 jit_solution(17442465708011333055)
XLA Ops:
  8.0 2.7 copy.8
  10.7 2.7 gather_fusion
  13.4 1.7 fusion.5
  15.0 2.6 collective-permute-start
  18.3 1.8 collective-permute-done
  20.1 3.1 fusion.2
  23.3 113.8 %reduce-scatter.2.cloned.1.call-done = f32[128,3,128]{0,2,1:T(8,128)} async-done(((f32[1024,3,128]{0,2,1:T(8,128)}), f32[128,3,128]{0,2,1:T(8,128)}) %reduce-scatter.2.cloned.1.call-update) | async-done | bytes 196624 | tf_op jit(solution)/shard_map/reduce_scatter | solution.py:36
  137.1 258.7 %all-gather.3.cloned.1.call-done = f32[8192,3,128]{0,2,1:T(8,128)} async-done(((f32[128,3,128]{0,2,1:T(8,128)}), f32[8192,3,128]{0,2,1:T(8,128)}) %all-gather.3.cloned.1.call-update) | async-done | bytes 12582928 | tf_op jit(solution)/shard_map/all_gather | solution.py:17
  395.9 17.4 %copy.13 = f32[8192,3,128]{2,1,0:T(4,128)} copy(f32[8192,3,128]{0,2,1:T(8,128)} %all-gather.3.cloned.1.call-done) | data formatting | bytes 25165824 | tf_op jit(solution)/shard_map/while | solution.py:23
  413.3 67.3 %while.10 = (s32[]{:T(128)}, f32[128,3,128]{2,1,0:T(4,128)S(1)}, s32[]{:T(128)}, f32[64,128,3,128]{3,2,1,0:T(4,128)}, s32[]{:T(128)}, /*index=5*/s32[]{:T(128)}, s32[]{:T(128)}) while((s32[]{:T(128)}, f32[128,3,128]{2,1,0:T(4,128)S(1)}, s32[]{:T(128)}, f32[64,128,3,128]{3,2,1,0:T(4,128)}, s32[]{:T(128)}, /*index=5*/s32[]{:T(128)}, ...), condition=%wide.region_2.3_spmd, body=%wide.region_1.2_spmd.sunk | while | flops 49157 | bytes 589939 | solution.py:23
  413.3 1.1 bitcast_add_fusion.2
  414.4 1.0 bitcast_add_fusion.2
  415.5 1.0 bitcast_add_fusion.2
  416.6 1.0 bitcast_add_fusion.2
  417.7 1.0 bitcast_add_fusion.2
  418.7 1.0 bitcast_add_fusion.2
  419.8 1.0 bitcast_add_fusion.2
  420.9 1.0 bitcast_add_fusion.2
  421.9 1.0 bitcast_add_fusion.2
  423.0 1.0 bitcast_add_fusion.2
  424.1 1.0 bitcast_add_fusion.2
  425.1 1.0 bitcast_add_fusion.2
  426.2 1.0 bitcast_add_fusion.2
  427.3 1.0 bitcast_add_fusion.2
  (64 shorter events, 53.5 us)
Async XLA Ops:
  6.5 13.5 %copy-start = (bf16[1,1024,1024]{2,1,0:T(8,128)(2,1)S(1)}, bf16[1,1024,1024]{2,1,0:T(8,128)(2,1)}, u32[]{:S(2)}) copy-start(bf16[1,1024,1024]{2,1,0:T(8,128)(2,1)} %param.6) | copy-start | bytes 6291460
  6.5 130.6 %reduce-scatter.2.cloned.1.call-start = ((), (), s32[]{:S(2)}) async-start(), calls=%async_computation.1 | async-start | bytes 1769472 | tf_op jit(solution)/shard_map/reduce_scatter | solution.py:36
  15.0 5.1 %collective-permute-start = (bf16[4,1024,128]{1,2,0:T(8,128)(2,1)}, bf16[4,1024,128]{1,2,0:T(8,128)(2,1)S(1)}, u32[]{:S(2)}, u32[]{:S(2)}) collective-permute-start(bf16[4,1024,128]{1,2,0:T(8,128)(2,1)} %fusion.5), channel_id=1, source_target_pairs={{8,0},{16,8},{24,16},{32,24},{40,32},{48,40},{56,48},{64,56},{72,6... | collective-permute-start | bytes 3145736 | tf_op jit(solution)/shard_map/ppermute | solution.py:12
  23.2 372.6 %all-gather.3.cloned.1.call-start = ((), (), s32[]{:S(2)}) async-start(), calls=%async_computation.2 | async-start | bytes 12779520 | tf_op jit(solution)/shard_map/all_gather | solution.py:17
  413.3 67.5 %copy-start.1 = (f32[128,3,128]{0,2,1:T(8,128)S(1)}, f32[128,3,128]{0,2,1:T(8,128)}, u32[]{:S(2)}) copy-start(f32[128,3,128]{0,2,1:T(8,128)} %reduce-scatter.2.cloned.1.call-done) | copy-start | bytes 589828
Sparse Core Ops, SparseCore 0:
  23.3 113.7 reduce-scatter.1
  141.4 254.4 all-gather.2
where the time goes:
time: 491 us; the launch traced here: 488 us
  waiting for transfers between devices  374 us (76%)
  other arithmetic  68.7 us (14%)
  local copies, waits for them, and re-layouts  23.7 us (5%)
  between operations  14.1 us (3%)
    all_gather x1, waiting for transfers between devices, carried_in(): gathered = lax.all_gather(part, axis)  259 us
    reduce_scatter x1, waiting for transfers between devices, local(): lax.psum_scatter(jnp.einsum('mc,tce->mte', tap_matrix, densities, preferr...  114 us
    add x63, other arithmetic, combine_sum(): return earlier + current  65.6 us
    while x2, local copies, waits for them, and re-layouts, carried_in(): return lax.fori_loop(0, place, one, state)  17.5 us
  transfers between devices with their start and end apart: 3, of which 3 were waited for; matrix products, arithmetic and copies ran while one was open for 0% of the time, Pallas kernels for 0%

commit v1 on v0

v1 whole, which is shorter than its diff:
```python
import functools

import jax
import jax.numpy as jnp
from jax import lax
from jax.experimental import pallas as pl
from jax.experimental.pallas import tpu as pltpu
from jax.sharding import PartitionSpec as P

MESH = pl.DeviceIdType.MESH
NX, NY = 4, 4
TICKS = 3
E = 128
HALVES = 2
HOP = 4
RELAY = 10
D2, D3, D4, D5 = 4, 8, 20, 24


def kernel(zl, off_ref, slots_ref, tap_hbm, dens_hbm, out_ref, tap, win, dmat, prod, rin, lin, gath, pre, tot, yin, exb, zout, zin,
           fin, res, rela, relb, loc, nb_s, nb_r, ca_s, ca_r, cb_s, cb_r, cd_s, cd_r, rs, rr, ls, lr, a_s, a_r, y_s, y_r, z_s, z_r,
           b_s, b_r):
    lag, p = lax.axis_index("lag"), lax.axis_index("col")
    core = lag % 2
    x = (lag // 2) % NX
    zh = (lag // (2 * NX)) % 2
    y = lag // (4 * NX)
    lanes = 2 * NX
    lane = x * 2 + core
    groups = TICKS * HALVES
    rows = prod.shape[2]
    piece = rows // lanes
    part = win.shape[1] // NX
    last = zl - 1

    def at(y_, zh_, x_, core_, p_):
        return (((y_ * 2 + zh_) * NX + x_) * 2 + core_, p_)

    def send(src, dst, ssem, rsem, to):
        return pltpu.make_async_remote_copy(src, dst, ssem, rsem, device_id=to, device_id_type=MESH)

    when = pl.when

    me = (lag, p)
    get_tap = pltpu.make_async_copy(tap_hbm, tap, loc.at[0])
    get_dens = pltpu.make_async_copy(dens_hbm, win.at[pl.ds(0, 4)], loc.at[1])
    get_dens.start()
    get_tap.start()

    cross_src = (x == 0) & (core == 0)
    cross_dst = (x == NX - 1) & (core == 1)
    final = lag == NY * 2 * lanes - 1

    def neighbour():
        return send(dens_hbm.at[pl.ds(0, 2)], win.at[pl.ds(4, 2)], nb_s.at[0], nb_r.at[0], (lag - 1, p))

    @when(jnp.logical_not(cross_src))
    def _():
        neighbour().start()

    def leg_a(j, way):
        k = 2 * j + way
        src = dens_hbm.at[k // NX, pl.ds((k % NX) * part, part)]
        return send(src, rela.at[way], ca_s.at[k], ca_r.at[way], at(y, zh, j, 1, p))

    sends_a = cross_src & (lag > 0)

    @when(sends_a)
    def _():
        for j in range(NX):
            for way in range(2):
                leg_a(j, way).start()

    z = zh * zl + p

    def leg_b(way):
        far = (z + (last if way == 0 else 2 * zl - last)) % (2 * zl)
        return send(rela.at[way], relb.at[way], cb_s.at[way], cb_r.at[way], at(y, far // zl, x, 1, far % zl))

    has_a = (core == 1) & ((y > 0) | (zh == 1))

    @when(has_a)
    def _():
        for way in range(2):
            leg_a(0, way).wait_recv()
            leg_b(way).start()

    def source_zh(way):
        return ((z + (2 * zl - last if way == 0 else last)) % (2 * zl)) // zl

    def has_b(way):
        return (core == 1) & ((y > 0) | (source_zh(way) == 1))

    def leg_d(way):
        to = (z + (1 if way == 0 else 2 * zl - 1)) % (2 * zl)
        y_to = y - (1 - source_zh(way))
        k = 2 * x + way
        dst = win.at[4 + k // NX, pl.ds((k % NX) * part, part)]
        return send(relb.at[way], dst, cd_s.at[way], cd_r.at[k], at(y_to, to // zl, NX - 1, 1, to % zl))

    def relay(mine):
        for way in range(2):

            @when(mine & has_b(way))
            def _(way=way):
                leg_b(way).wait_recv()
                leg_d(way).start()

    relay(x == NX - 1)

    @when(final)
    def _():
        win[pl.ds(4, 2)] = jnp.zeros((2, *win.shape[1:]), win.dtype)

    get_dens.wait()

    @when(jnp.logical_not(cross_dst))
    def _():
        neighbour().wait_recv()

    @when(cross_dst & jnp.logical_not(final))
    def _():
        for k in range(2 * NX):
            dst = win.at[4 + k // NX, pl.ds((k % NX) * part, part)]
            send(relb.at[0], dst, cd_s.at[0], cd_r.at[k], me).wait_recv()

    perm = (lax.broadcasted_iota(jnp.int32, (E, E), 0) == slots_ref[...]).astype(jnp.float32).astype(jnp.bfloat16)
    first = off_ref[0]
    for t in range(TICKS):
        dmat[:, t * E : (t + 1) * E] = jnp.dot(win[first + t], perm, preferred_element_type=jnp.float32).astype(jnp.bfloat16)
    get_tap.wait()
    chunk = rows * HALVES

    def product(d, _):
        block = jnp.dot(tap[pl.ds(pl.multiple_of(d * chunk, chunk), chunk), :], dmat[...], preferred_element_type=jnp.float32)
        for t in range(TICKS):
            for h in range(HALVES):
                prod[d, t * HALVES + h] = block[h * rows : (h + 1) * rows, t * E : (t + 1) * E]
        return 0

    lax.fori_loop(0, zl, product, 0)

    def move(step, hops, sign, buf, ssem, rsem):
        n = step - HOP * hops
        count = jnp.where(hops == 0, last, zl - hops) * groups

        @when((n >= 0) & (n < count))
        def _():
            i = n // groups
            g = n % groups
            d = last - i if sign > 0 else i

            @when(hops > 0)
            def _():
                send(prod.at[d, g], buf.at[d, g], ssem.at[d, g], rsem.at[d, g], me).wait_recv()
                prod[d, g] = prod[d, g] + buf[d, g]

            @when(d != p)
            def _():
                send(prod.at[d, g], buf.at[d, g], ssem.at[d, g], rsem.at[d, g], (lag, p + sign)).start()

    def peers(body):
        for j in range(lanes):

            @when(j != lane)
            def _(j=j):
                body(j)

    def mine(j):
        return pl.ds(j * piece, piece)

    def lane_at(j):
        return at(y, zh, j // 2, j % 2, p)

    def out_copy(g, j):
        return send(prod.at[p, g, mine(j)], gath.at[g, lane], a_s.at[g, j], a_r.at[g, lane], lane_at(j))

    def back_copy(g, j):
        return send(fin.at[g, j], res.at[g, mine(lane)], b_s.at[g, j], b_r.at[g, lane], lane_at(j))

    def y_copy(g, j):
        return send(tot.at[g], yin.at[g, y], y_s.at[g, j], y_r.at[g, y], at(j, zh, x, core, p))

    def z_copy(g):
        return send(zout.at[g], zin.at[g], z_s.at[g], z_r.at[g], at(y, 1 - zh, x, core, p))

    def stage1(g):
        gath[g, lane] = prod[p, g, pl.ds(pl.multiple_of(lane * piece, piece), piece)]
        peers(lambda j: out_copy(g, j).start())

    def stage2(g):
        peers(lambda j: send(prod.at[p, g, mine(j)], gath.at[g, j], a_s.at[g, j], a_r.at[g, j], me).wait_recv())
        c = gath[g, 0]
        pre[g, 0] = c
        for j in range(1, lanes):
            c = c + gath[g, j]
            pre[g, j] = c
        tot[g] = c
        for j in range(1, NY):

            @when(j > y)
            def _(j=j):
                y_copy(g, j).start()

    def stage3(g):
        exb[g] = jnp.zeros(exb.shape[1:], exb.dtype)
        for j in range(NY - 1):

            @when(j < y)
            def _(j=j):
                send(tot.at[g], yin.at[g, j], y_s.at[g, j], y_r.at[g, j], me).wait_recv()
                exb[g] = exb[g] + yin[g, j]

        zout[g] = exb[g] + jnp.where(zh == 0, tot[g], 0.0)
        z_copy(g).start()

    def stage4(g):
        z_copy(g).wait_recv()
        e = exb[g] + zin[g]
        for j in range(lanes):
            fin[g, j] = pre[g, j] + e
        res[g, pl.ds(pl.multiple_of(lane * piece, piece), piece)] = fin[g, lane]
        peers(lambda j: back_copy(g, j).start())

    def stage5(g):
        peers(lambda j: send(fin.at[g, j], res.at[g, mine(j)], b_s.at[g, j], b_r.at[g, j], me).wait_recv())
        out_ref[g // HALVES, pl.ds(pl.multiple_of((g % HALVES) * rows, rows), rows)] = res[g]

    def ready(q):
        right = jnp.where(q > 0, HOP * q + (last - q) * groups, 0)
        left = jnp.where(q < last, HOP * (last - q) + q * groups, 0)
        return jnp.maximum(right, left)

    base = ready(p)
    longest = max(max(HOP * q + (last - q) * groups if q else 0, HOP * (last - q) + q * groups if q < last else 0) for q in range(zl))

    def step(s, _):
        move(s, p, 1, rin, rs, rr)
        move(s, last - p, -1, lin, ls, lr)

        @when(s == RELAY)
        def _():
            relay(x < NX - 1)

        for delay, stage in ((0, stage1), (D2, stage2), (D3, stage3), (D4, stage4), (D5, stage5)):
            g = s - base - delay

            @when((g >= 0) & (g < groups))
            def _(g=g, stage=stage):
                stage(g)

        return 0

    lax.fori_loop(0, longest + groups + D5, step, 0)

    @when(jnp.logical_not(cross_src))
    def _():
        neighbour().wait_send()

    @when(sends_a)
    def _():
        for j in range(NX):
            for way in range(2):
                leg_a(j, way).wait_send()

    @when(has_a)
    def _():
        for way in range(2):
            leg_b(way).wait_send()

    for way in range(2):

        @when(has_b(way))
        def _(way=way):
            leg_d(way).wait_send()

    def drain(d, _):
        def one(g, _):
            @when(d > p)
            def _():
                send(prod.at[d, g], rin.at[d, g], rs.at[d, g], rr.at[d, g], me).wait_send()

            @when(d < p)
            def _():
                send(prod.at[d, g], lin.at[d, g], ls.at[d, g], lr.at[d, g], me).wait_send()

            return 0

        return lax.fori_loop(0, groups, one, 0)

    lax.fori_loop(0, zl, drain, 0)

    def drain_scan(g, _):
        peers(lambda j: out_copy(g, j).wait_send())
        peers(lambda j: back_copy(g, j).wait_send())
        for j in range(1, NY):

            @when(j > y)
            def _(j=j):
                y_copy(g, j).wait_send()

        z_copy(g).wait_send()
        return 0

    lax.fori_loop(0, groups, drain_scan, 0)


def local(zl, tap_matrices, density_history, offsets, column_slots):
    m, c = tap_matrices.shape[1:]
    chunk = m // zl
    groups, rows, lanes = TICKS * HALVES, chunk // HALVES, 2 * NX
    piece, part = rows // lanes, c // NX
    f32, bf16 = jnp.float32, jnp.bfloat16
    vmem, dma = pltpu.VMEM, pltpu.SemaphoreType.DMA
    out = pl.pallas_call(
        functools.partial(kernel, zl),
        out_shape=jax.ShapeDtypeStruct((TICKS, chunk, E), f32),
        in_specs=[
            pl.BlockSpec(memory_space=pltpu.SMEM),
            pl.BlockSpec(memory_space=pltpu.VMEM),
            pl.BlockSpec(memory_space=pl.ANY),
            pl.BlockSpec(memory_space=pl.ANY),
        ],
        out_specs=pl.BlockSpec(memory_space=pltpu.VMEM),
        scratch_shapes=[
            vmem((m, c), bf16),
            vmem((6, c, E), bf16),
            vmem((c, TICKS * E), bf16),
            vmem((zl, groups, rows, E), f32),
            vmem((zl, groups, rows, E), f32),
            vmem((zl, groups, rows, E), f32),
            vmem((groups, lanes, piece, E), f32),
            vmem((groups, lanes, piece, E), f32),
            vmem((groups, piece, E), f32),
            vmem((groups, NY, piece, E), f32),
            vmem((groups, piece, E), f32),
            vmem((groups, piece, E), f32),
            vmem((groups, piece, E), f32),
            vmem((groups, lanes, piece, E), f32),
            vmem((groups, rows, E), f32),
            vmem((2, part, E), bf16),
            vmem((2, part, E), bf16),
            dma((2,)),
            dma((1,)), dma((1,)),
            dma((2 * NX,)), dma((2,)),
            dma((2,)), dma((2,)),
            dma((2,)), dma((2 * NX,)),
            dma((zl, groups)), dma((zl, groups)),
            dma((zl, groups)), dma((zl, groups)),
            dma((groups, lanes)), dma((groups, lanes)),
            dma((groups, NY)), dma((groups, NY)),
            dma((groups,)), dma((groups,)),
            dma((groups, lanes)), dma((groups, lanes)),
        ],
        compiler_params=pltpu.CompilerParams(has_side_effects=True, vmem_limit_bytes=40 << 20),
    )(offsets, column_slots, tap_matrices.reshape(m, c), density_history)
    return out.transpose(1, 0, 2)[None]


def solution(mesh):
    return jax.shard_map(
        functools.partial(local, mesh.shape["col"]),
        mesh=mesh,
        in_specs=(P("lag", None, "col"), P("lag", "col", None), P("lag"), P("col", None)),
        out_specs=P("lag", "col", None, None),
        check_vma=False,
    )
```

time: 491 us -> 108 us (0.22)
  the two profiles are of different devices: /device:TPU:479 before, /device:TPU:33 now
where the time goes in v1:
time: 108 us
  Pallas kernels  103 us (95%)
  local copies, waits for them, and re-layouts  4.14 us (4%)
    pallas_call x1, Pallas kernels, local(): pl.pallas_call(functools.partial(kernel, zl), out_shape=jax.ShapeDtypeStr...  103 us
    unnamed x7, local copies, waits for them, and re-layouts  4.14 us

profile of v1, /device:TPU:33, one launch (start us, length us, event | category | flops | bytes accessed | tf_op | source)
XLA Modules:
  0.0 107.8 jit_solution(4494282128974191388)
XLA Ops:
  0.7 0.0 copy-start
  0.7 1.6 %copy-done = bf16[1,1024,1024]{2,1,0:T(8,128)(2,1)S(1)} copy-done((bf16[1,1024,1024]{2,1,0:T(8,128)(2,1)S(1)}, bf16[1,1024,1024]{2,1,0:T(8,128)(2,1)}, u32[]{:S(2)}) %copy-start) | copy-done | bytes 2097176
  2.2 0.0 copy-start.1
  2.2 1.2 %copy-done.1 = bf16[4,1024,128]{2,1,0:T(8,128)(2,1)S(1)} copy-done((bf16[4,1024,128]{2,1,0:T(8,128)(2,1)S(1)}, bf16[4,1024,128]{2,1,0:T(8,128)(2,1)}, u32[]{:S(2)}) %copy-start.1) | copy-done | bytes 1048600
  3.5 0.0 copy-start.2
  3.5 0.7 copy-done.2
  4.1 103.0 %shard_map.46 = f32[3,128,128]{2,1,0:T(8,128)S(1)} custom-call(s32[1]{0:T(128)S(6)} %copy.6.off_ref, s32[1,128]{1,0:T(1,128)S(1)} %copy-done.2, bf16[1024,1024]{1,0:T(8,128)(2,1)S(1)} %bitcast.4, bf16[4,1024,128]{2,1,0:T(8,128)(2,1)S(1)} %copy-done.1), custom_call_target="tpu_custom_call" | custom-call | tf_op jit(solution)/shard_map/pallas_call | solution.py:315
  107.1 0.7 copy.7
Async XLA Ops:
  0.7 1.6 %copy-start = (bf16[1,1024,1024]{2,1,0:T(8,128)(2,1)S(1)}, bf16[1,1024,1024]{2,1,0:T(8,128)(2,1)}, u32[]{:S(2)}) copy-start(bf16[1,1024,1024]{2,1,0:T(8,128)(2,1)} %param.4) | copy-start | bytes 6291460
  2.2 1.2 %copy-start.1 = (bf16[4,1024,128]{2,1,0:T(8,128)(2,1)S(1)}, bf16[4,1024,128]{2,1,0:T(8,128)(2,1)}, u32[]{:S(2)}) copy-start(bf16[4,1024,128]{2,1,0:T(8,128)(2,1)} %dens_hbm.1) | copy-start | bytes 3145732
  3.5 0.7 copy-start.2

commit v2 on v1

--- a/solution.py
+++ b/solution.py
@@ -12,13 +12,12 @@
 TICKS = 3
 E = 128
 HALVES = 2
-HOP = 4
-RELAY = 10
-D2, D3, D4, D5 = 4, 8, 20, 24
-
-
-def kernel(zl, off_ref, slots_ref, tap_hbm, dens_hbm, out_ref, tap, win, dmat, prod, rin, lin, gath, pre, tot, yin, exb, zout, zin,
-           fin, res, rela, relb, loc, nb_s, nb_r, ca_s, ca_r, cb_s, cb_r, cd_s, cd_r, rs, rr, ls, lr, a_s, a_r, y_s, y_r, z_s, z_r,
+HOP = 6
+D2, D3, D4, D5 = 8, 16, 32, 40
+
+
+def kernel(zl, off_ref, slots_hbm, tap_hbm, dens_hbm, out_ref, slots_ref, tap, win, dmat, prod, rin, lin, gath, pre, tot, yin, exb, zout, zin,
+           fin, res, rela, loc, nb_s, nb_r, ca_s, ca_r, cb_s, cb_r, hello, rs, rr, ls, lr, a_s, a_r, y_s, y_r, z_s, z_r,
            b_s, b_r):
     lag, p = lax.axis_index("lag"), lax.axis_index("col")
     core = lag % 2
@@ -30,7 +29,7 @@
     groups = TICKS * HALVES
     rows = prod.shape[2]
     piece = rows // lanes
-    part = win.shape[1] // NX
+    part = win.shape[1] // (NX // 2)
     last = zl - 1
 
     def at(y_, zh_, x_, core_, p_):
@@ -44,12 +43,63 @@
     me = (lag, p)
     get_tap = pltpu.make_async_copy(tap_hbm, tap, loc.at[0])
     get_dens = pltpu.make_async_copy(dens_hbm, win.at[pl.ds(0, 4)], loc.at[1])
+    get_slots = pltpu.make_async_copy(slots_hbm, slots_ref, loc.at[2])
     get_dens.start()
     get_tap.start()
+    get_slots.start()
+    z = zh * zl + p
+
+    def round_z(q):
+        q = (q + 2 * zl) % (2 * zl)
+        return q // zl, q % zl
 
     cross_src = (x == 0) & (core == 0)
     cross_dst = (x == NX - 1) & (core == 1)
     final = lag == NY * 2 * lanes - 1
+    sends_a = cross_src & (lag > 0)
+    has_a = (core == 1) & ((y > 0) | (zh == 1))
+
+    def middle(zh_):
+        return (core == 1) & ((y > 0) | (zh_ == 1))
+
+    barrier = pltpu.get_barrier_semaphore()
+
+    def greet(to):
+        pl.semaphore_signal(barrier, inc=1, device_id=to, device_id_type=MESH)
+
+    for j in range(lanes):
+
+        @when(j != lane)
+        def _(j=j):
+            greet(at(y, zh, j // 2, j % 2, p))
+
+    @when(p > 0)
+    def _():
+        greet((lag, p - 1))
+
+    @when(p < last)
+    def _():
+        greet((lag, p + 1))
+
+    for j in range(NY - 1):
+
+        @when(j < y)
+        def _(j=j):
+            greet(at(j, zh, x, core, p))
+
+    ahead, behind = round_z(z + zl // 2), round_z(z - zl // 2)
+    greet(at(y, ahead[0], x, core, ahead[1]))
+    greet(at(y, behind[0], x, core, behind[1]))
+
+    @when(cross_dst & jnp.logical_not(final))
+    def _():
+        for j in range(NX):
+            greet(at(y + zh, ahead[0], j, 1, ahead[1]))
+
+    one = lambda c: c.astype(jnp.int32)
+    many = lanes - 1 + one(p > 0) + one(p < last) + NY - 1 - y + 2 + one(middle(ahead[0]))
+    pl.semaphore_wait(barrier, many)
+    pl.semaphore_signal(hello, inc=1, device_id=at(y, ahead[0], x, core, ahead[1]), device_id_type=MESH)
 
     def neighbour():
         return send(dens_hbm.at[pl.ds(0, 2)], win.at[pl.ds(4, 2)], nb_s.at[0], nb_r.at[0], (lag - 1, p))
@@ -58,55 +108,26 @@
     def _():
         neighbour().start()
 
-    def leg_a(j, way):
-        k = 2 * j + way
-        src = dens_hbm.at[k // NX, pl.ds((k % NX) * part, part)]
-        return send(src, rela.at[way], ca_s.at[k], ca_r.at[way], at(y, zh, j, 1, p))
-
-    sends_a = cross_src & (lag > 0)
+    def part_of(ref, j, first):
+        return ref.at[first + j // (NX // 2), pl.ds((j % (NX // 2)) * part, part)]
+
+    def leg_a(j):
+        return send(part_of(dens_hbm, j, 0), rela, ca_s.at[j], ca_r.at[0], at(y, zh, j, 1, p))
+
+    def leg_b():
+        return send(rela, part_of(win, x, 4), cb_s.at[0], cb_r.at[x], at(y - (1 - zh), 1 - zh, NX - 1, 1, p))
 
     @when(sends_a)
     def _():
         for j in range(NX):
-            for way in range(2):
-                leg_a(j, way).start()
-
-    z = zh * zl + p
-
-    def leg_b(way):
-        far = (z + (last if way == 0 else 2 * zl - last)) % (2 * zl)
-        return send(rela.at[way], relb.at[way], cb_s.at[way], cb_r.at[way], at(y, far // zl, x, 1, far % zl))
-
-    has_a = (core == 1) & ((y > 0) | (zh == 1))
+            leg_a(j).start()
+
+    pl.semaphore_wait(hello, 1)
 
     @when(has_a)
     def _():
-        for way in range(2):
-            leg_a(0, way).wait_recv()
-            leg_b(way).start()
-
-    def source_zh(way):
-        return ((z + (2 * zl - last if way == 0 else last)) % (2 * zl)) // zl
-
-    def has_b(way):
-        return (core == 1) & ((y > 0) | (source_zh(way) == 1))
-
-    def leg_d(way):
-        to = (z + (1 if way == 0 else 2 * zl - 1)) % (2 * zl)
-        y_to = y - (1 - source_zh(way))
-        k = 2 * x + way
-        dst = win.at[4 + k // NX, pl.ds((k % NX) * part, part)]
-        return send(relb.at[way], dst, cd_s.at[way], cd_r.at[k], at(y_to, to // zl, NX - 1, 1, to % zl))
-
-    def relay(mine):
-        for way in range(2):
-
-            @when(mine & has_b(way))
-            def _(way=way):
-                leg_b(way).wait_recv()
-                leg_d(way).start()
-
-    relay(x == NX - 1)
+        leg_a(0).wait_recv()
+        leg_b().start()
 
     @when(final)
     def _():
@@ -120,10 +141,10 @@
 
     @when(cross_dst & jnp.logical_not(final))
     def _():
-        for k in range(2 * NX):
-            dst = win.at[4 + k // NX, pl.ds((k % NX) * part, part)]
-            send(relb.at[0], dst, cd_s.at[0], cd_r.at[k], me).wait_recv()
-
+        for j in range(NX):
+            send(rela, part_of(win, j, 4), cb_s.at[0], cb_r.at[j], me).wait_recv()
+
+    get_slots.wait()
     perm = (lax.broadcasted_iota(jnp.int32, (E, E), 0) == slots_ref[...]).astype(jnp.float32).astype(jnp.bfloat16)
     first = off_ref[0]
     for t in range(TICKS):
@@ -131,14 +152,18 @@
     get_tap.wait()
     chunk = rows * HALVES
 
-    def product(d, _):
+    def product(k):
+        d = jnp.where(k % 2 == 0, last - k // 2, k // 2)
         block = jnp.dot(tap[pl.ds(pl.multiple_of(d * chunk, chunk), chunk), :], dmat[...], preferred_element_type=jnp.float32)
         for t in range(TICKS):
             for h in range(HALVES):
                 prod[d, t * HALVES + h] = block[h * rows : (h + 1) * rows, t * E : (t + 1) * E]
+
+    def first_two(k, _):
+        product(k)
         return 0
 
-    lax.fori_loop(0, zl, product, 0)
+    lax.fori_loop(0, 2, first_two, 0)
 
     def move(step, hops, sign, buf, ssem, rsem):
         n = step - HOP * hops
@@ -238,9 +263,9 @@
         move(s, p, 1, rin, rs, rr)
         move(s, last - p, -1, lin, ls, lr)
 
-        @when(s == RELAY)
+        @when(s < zl - 2)
         def _():
-            relay(x < NX - 1)
+            product(s + 2)
 
         for delay, stage in ((0, stage1), (D2, stage2), (D3, stage3), (D4, stage4), (D5, stage5)):
             g = s - base - delay
@@ -260,19 +285,11 @@
     @when(sends_a)
     def _():
         for j in range(NX):
-            for way in range(2):
-                leg_a(j, way).wait_send()
+            leg_a(j).wait_send()
 
     @when(has_a)
     def _():
-        for way in range(2):
-            leg_b(way).wait_send()
-
-    for way in range(2):
-
-        @when(has_b(way))
-        def _(way=way):
-            leg_d(way).wait_send()
+        leg_b().wait_send()
 
     def drain(d, _):
         def one(g, _):
@@ -309,7 +326,7 @@
     m, c = tap_matrices.shape[1:]
     chunk = m // zl
     groups, rows, lanes = TICKS * HALVES, chunk // HALVES, 2 * NX
-    piece, part = rows // lanes, c // NX
+    piece, part = rows // lanes, c // (NX // 2)
     f32, bf16 = jnp.float32, jnp.bfloat16
     vmem, dma = pltpu.VMEM, pltpu.SemaphoreType.DMA
     out = pl.pallas_call(
@@ -317,12 +334,13 @@
         out_shape=jax.ShapeDtypeStruct((TICKS, chunk, E), f32),
         in_specs=[
             pl.BlockSpec(memory_space=pltpu.SMEM),
-            pl.BlockSpec(memory_space=pltpu.VMEM),
+            pl.BlockSpec(memory_space=pl.ANY),
             pl.BlockSpec(memory_space=pl.ANY),
             pl.BlockSpec(memory_space=pl.ANY),
         ],
         out_specs=pl.BlockSpec(memory_space=pltpu.VMEM),
         scratch_shapes=[
+            vmem((1, E), jnp.int32),
             vmem((m, c), bf16),
             vmem((6, c, E), bf16),
             vmem((c, TICKS * E), bf16),
@@ -338,13 +356,12 @@
             vmem((groups, piece, E), f32),
             vmem((groups, lanes, piece, E), f32),
             vmem((groups, rows, E), f32),
-            vmem((2, part, E), bf16),
-            vmem((2, part, E), bf16),
-            dma((2,)),
+            vmem((part, E), bf16),
+            dma((3,)),
             dma((1,)), dma((1,)),
-            dma((2 * NX,)), dma((2,)),
-            dma((2,)), dma((2,)),
-            dma((2,)), dma((2 * NX,)),
+            dma((NX,)), dma((1,)),
+            dma((1,)), dma((NX,)),
+            pltpu.SemaphoreType.REGULAR,
             dma((zl, groups)), dma((zl, groups)),
             dma((zl, groups)), dma((zl, groups)),
             dma((groups, lanes)), dma((groups, lanes)),
@@ -352,7 +369,7 @@
             dma((groups,)), dma((groups,)),
             dma((groups, lanes)), dma((groups, lanes)),
         ],
-        compiler_params=pltpu.CompilerParams(has_side_effects=True, vmem_limit_bytes=40 << 20),
+        compiler_params=pltpu.CompilerParams(collective_id=0, has_side_effects=True, vmem_limit_bytes=62 << 20),
     )(offsets, column_slots, tap_matrices.reshape(m, c), density_history)
     return out.transpose(1, 0, 2)[None]
 

time: 108 us -> 78.5 us (0.73)
  the two profiles are of different devices: /device:TPU:33 before, /device:TPU:25 now
where the time goes in v2:
time: 78.5 us; the launch traced here: 78.1 us
  Pallas kernels  75.8 us (97%)
  local copies, waits for them, and re-layouts  1.62 us (2%)
    pallas_call x1, Pallas kernels, local(): pl.pallas_call(functools.partial(kernel, zl), out_shape=jax.ShapeDtypeStr...  75.8 us
    unnamed x1, local copies, waits for them, and re-layouts  1.62 us

profile of v2, /device:TPU:25, one launch (start us, length us, event | category | flops | bytes accessed | tf_op | source)
XLA Modules:
  0.0 78.1 jit_solution(2245923003886814452)
XLA Ops:
  0.7 75.8 %shard_map.46 = f32[3,128,128]{2,1,0:T(8,128)} custom-call(s32[1]{0:T(128)S(6)} %copy.6.off_ref, s32[1,128]{1,0:T(1,128)} %slots_hbm.1, bf16[1024,1024]{1,0:T(8,128)(2,1)} %bitcast.4, bf16[4,1024,128]{2,1,0:T(8,128)(2,1)} %dens_hbm.1), custom_call_target="tpu_custom_call" | custom-call | tf_op jit(solution)/shard_map/pallas_call | solution.py:332
  76.5 1.6 %copy.7 = f32[1,128,3,128]{3,1,2,0:T(8,128)} copy(f32[1,128,3,128]{3,1,2,0:T(8,128)} %bitcast.5) | data formatting | bytes 393216

commit v3 on v2

--- a/solution.py
+++ b/solution.py
@@ -13,7 +13,7 @@
 E = 128
 HALVES = 2
 HOP = 6
-D2, D3, D4, D5 = 8, 16, 32, 40
+D2, D3, D4, D5 = 7, 14, 29, 36
 
 
 def kernel(zl, off_ref, slots_hbm, tap_hbm, dens_hbm, out_ref, slots_ref, tap, win, dmat, prod, rin, lin, gath, pre, tot, yin, exb, zout, zin,
@@ -59,19 +59,22 @@
     sends_a = cross_src & (lag > 0)
     has_a = (core == 1) & ((y > 0) | (zh == 1))
 
-    def middle(zh_):
-        return (core == 1) & ((y > 0) | (zh_ == 1))
-
     barrier = pltpu.get_barrier_semaphore()
 
     def greet(to):
         pl.semaphore_signal(barrier, inc=1, device_id=to, device_id_type=MESH)
 
-    for j in range(lanes):
-
-        @when(j != lane)
-        def _(j=j):
-            greet(at(y, zh, j // 2, j % 2, p))
+    def loop(count, body):
+        def one_more(j, _):
+            body(j)
+            return 0
+
+        lax.fori_loop(0, count, one_more, 0)
+
+    def others(body):
+        loop(lanes - 1, lambda j: body((lane + 1 + j) % lanes))
+
+    others(lambda j: greet(at(y, zh, j // 2, j % 2, p)))
 
     @when(p > 0)
     def _():
@@ -81,25 +84,36 @@
     def _():
         greet((lag, p + 1))
 
-    for j in range(NY - 1):
-
-        @when(j < y)
-        def _(j=j):
-            greet(at(j, zh, x, core, p))
-
-    ahead, behind = round_z(z + zl // 2), round_z(z - zl // 2)
-    greet(at(y, ahead[0], x, core, ahead[1]))
-    greet(at(y, behind[0], x, core, behind[1]))
+    loop(y, lambda j: greet(at(j, zh, x, core, p)))
+
+    eighth, quarter = zl // 4, zl // 2
+
+    def along(dz):
+        zh_, p_ = round_z(z + dz)
+        return at(y, zh_, x, core, p_)
+
+    greet(along(eighth))
+    greet(along(-eighth))
 
     @when(cross_dst & jnp.logical_not(final))
     def _():
+        zh_, p_ = round_z(z - eighth)
         for j in range(NX):
-            greet(at(y + zh, ahead[0], j, 1, ahead[1]))
+            greet(at(y + zh, zh_, j, 1, p_))
 
     one = lambda c: c.astype(jnp.int32)
-    many = lanes - 1 + one(p > 0) + one(p < last) + NY - 1 - y + 2 + one(middle(ahead[0]))
+    far = round_z(z + eighth)[0]
+    many = lanes - 1 + one(p > 0) + one(p < last) + NY - 1 - y + 2 + one((core == 1) & ((y > 0) | (far == 0)))
     pl.semaphore_wait(barrier, many)
-    pl.semaphore_signal(hello, inc=1, device_id=at(y, ahead[0], x, core, ahead[1]), device_id_type=MESH)
+    for dz in (eighth, -eighth):
+        pl.semaphore_signal(hello.at[0], inc=1, device_id=along(dz), device_id_type=MESH)
+
+    def vouch():
+        pl.semaphore_wait(hello.at[0], 2)
+        pl.semaphore_signal(hello.at[1], inc=1, device_id=along(-quarter), device_id_type=MESH)
+
+    def vouched():
+        pl.semaphore_wait(hello.at[1], 1)
 
     def neighbour():
         return send(dens_hbm.at[pl.ds(0, 2)], win.at[pl.ds(4, 2)], nb_s.at[0], nb_r.at[0], (lag - 1, p))
@@ -122,7 +136,10 @@
         for j in range(NX):
             leg_a(j).start()
 
-    pl.semaphore_wait(hello, 1)
+    @when(core == 1)
+    def _():
+        vouch()
+        vouched()
 
     @when(has_a)
     def _():
@@ -159,82 +176,85 @@
             for h in range(HALVES):
                 prod[d, t * HALVES + h] = block[h * rows : (h + 1) * rows, t * E : (t + 1) * E]
 
-    def first_two(k, _):
-        product(k)
-        return 0
-
-    lax.fori_loop(0, 2, first_two, 0)
+    @when(core == 0)
+    def _():
+        vouch()
 
     def move(step, hops, sign, buf, ssem, rsem):
+        def copy(d, g, to):
+            return send(prod.at[d, g], buf.at[d, g], ssem.at[d], rsem.at[d, g], to)
+
+        @when((hops == 0) & (step < last))
+        def _():
+            d = last - step if sign > 0 else step
+            loop(groups, lambda g: copy(d, g, (lag, p + sign)).start())
+
         n = step - HOP * hops
-        count = jnp.where(hops == 0, last, zl - hops) * groups
-
-        @when((n >= 0) & (n < count))
+
+        @when((hops > 0) & (n >= 0) & (n < (zl - hops) * groups))
         def _():
             i = n // groups
             g = n % groups
             d = last - i if sign > 0 else i
-
-            @when(hops > 0)
-            def _():
-                send(prod.at[d, g], buf.at[d, g], ssem.at[d, g], rsem.at[d, g], me).wait_recv()
-                prod[d, g] = prod[d, g] + buf[d, g]
+            copy(d, g, me).wait_recv()
+            prod[d, g] = prod[d, g] + buf[d, g]
 
             @when(d != p)
             def _():
-                send(prod.at[d, g], buf.at[d, g], ssem.at[d, g], rsem.at[d, g], (lag, p + sign)).start()
-
-    def peers(body):
-        for j in range(lanes):
-
-            @when(j != lane)
-            def _(j=j):
-                body(j)
+                copy(d, g, (lag, p + sign)).start()
 
     def mine(j):
-        return pl.ds(j * piece, piece)
+        return pl.ds(pl.multiple_of(j * piece, piece), piece)
 
     def lane_at(j):
         return at(y, zh, j // 2, j % 2, p)
 
     def out_copy(g, j):
-        return send(prod.at[p, g, mine(j)], gath.at[g, lane], a_s.at[g, j], a_r.at[g, lane], lane_at(j))
+        return send(prod.at[p, g, mine(j)], gath.at[g, lane], a_s.at[g], a_r.at[g], lane_at(j))
 
     def back_copy(g, j):
-        return send(fin.at[g, j], res.at[g, mine(lane)], b_s.at[g, j], b_r.at[g, lane], lane_at(j))
+        return send(fin.at[g, j], res.at[g, mine(lane)], b_s.at[g], b_r.at[g], lane_at(j))
 
     def y_copy(g, j):
-        return send(tot.at[g], yin.at[g, y], y_s.at[g, j], y_r.at[g, y], at(j, zh, x, core, p))
+        return send(tot.at[g], yin.at[g, y], y_s.at[g], y_r.at[g], at(j, zh, x, core, p))
 
     def z_copy(g):
         return send(zout.at[g], zin.at[g], z_s.at[g], z_r.at[g], at(y, 1 - zh, x, core, p))
 
+    def all_of(g, sems, rsems, count):
+        some = gath.at[g, pl.ds(0, count)]
+        return send(some, some, sems.at[g], rsems.at[g], me)
+
     def stage1(g):
-        gath[g, lane] = prod[p, g, pl.ds(pl.multiple_of(lane * piece, piece), piece)]
-        peers(lambda j: out_copy(g, j).start())
+        gath[g, lane] = prod[p, g, mine(lane)]
+        others(lambda j: out_copy(g, j).start())
 
     def stage2(g):
-        peers(lambda j: send(prod.at[p, g, mine(j)], gath.at[g, j], a_s.at[g, j], a_r.at[g, j], me).wait_recv())
+        all_of(g, a_s, a_r, lanes - 1).wait_recv()
         c = gath[g, 0]
         pre[g, 0] = c
         for j in range(1, lanes):
             c = c + gath[g, j]
             pre[g, j] = c
         tot[g] = c
-        for j in range(1, NY):
-
-            @when(j > y)
-            def _(j=j):
-                y_copy(g, j).start()
+        loop(NY - 1 - y, lambda j: y_copy(g, y + 1 + j).start())
 
     def stage3(g):
         exb[g] = jnp.zeros(exb.shape[1:], exb.dtype)
-        for j in range(NY - 1):
-
-            @when(j < y)
-            def _(j=j):
-                send(tot.at[g], yin.at[g, j], y_s.at[g, j], y_r.at[g, j], me).wait_recv()
-                exb[g] = exb[g] + yin[g, j]
+        for q in range(1, NY):
+
+            @when(y == q)
+            def _(q=q):
+                all_of(g, y_s, y_r, q).wait_recv()
+
+        def add(j):
+            exb[g] = exb[g] + yin[g, j]
+
+        loop(y, add)
+
+        @when((core == 0) & (g == 0))
+        def _():
+            vouched()
 
         zout[g] = exb[g] + jnp.where(zh == 0, tot[g], 0.0)
         z_copy(g).start()
@@ -244,11 +264,11 @@
         e = exb[g] + zin[g]
         for j in range(lanes):
             fin[g, j] = pre[g, j] + e
-        res[g, pl.ds(pl.multiple_of(lane * piece, piece), piece)] = fin[g, lane]
-        peers(lambda j: back_copy(g, j).start())
+        res[g, mine(lane)] = fin[g, lane]
+        others(lambda j: back_copy(g, j).start())
 
     def stage5(g):
-        peers(lambda j: send(fin.at[g, j], res.at[g, mine(j)], b_s.at[g, j], b_r.at[g, j], me).wait_recv())
+        all_of(g, b_s, b_r, lanes - 1).wait_recv()
         out_ref[g // HALVES, pl.ds(pl.multiple_of((g % HALVES) * rows, rows), rows)] = res[g]
 
     def ready(q):
@@ -260,12 +280,12 @@
     longest = max(max(HOP * q + (last - q) * groups if q else 0, HOP * (last - q) + q * groups if q < last else 0) for q in range(zl))
 
     def step(s, _):
+        @when(s < zl // 2)
+        def _():
+            loop(2, lambda k: product(2 * s + k))
+
         move(s, p, 1, rin, rs, rr)
         move(s, last - p, -1, lin, ls, lr)
-
-        @when(s < zl - 2)
-        def _():
-            product(s + 2)
 
         for delay, stage in ((0, stage1), (D2, stage2), (D3, stage3), (D4, stage4), (D5, stage5)):
             g = s - base - delay
@@ -291,35 +311,31 @@
     def _():
         leg_b().wait_send()
 
-    def drain(d, _):
-        def one(g, _):
-            @when(d > p)
-            def _():
-                send(prod.at[d, g], rin.at[d, g], rs.at[d, g], rr.at[d, g], me).wait_send()
-
-            @when(d < p)
-            def _():
-                send(prod.at[d, g], lin.at[d, g], ls.at[d, g], lr.at[d, g], me).wait_send()
-
-            return 0
-
-        return lax.fori_loop(0, groups, one, 0)
-
-    lax.fori_loop(0, zl, drain, 0)
-
-    def drain_scan(g, _):
-        peers(lambda j: out_copy(g, j).wait_send())
-        peers(lambda j: back_copy(g, j).wait_send())
-        for j in range(1, NY):
-
-            @when(j > y)
-            def _(j=j):
-                y_copy(g, j).wait_send()
+    def drain(d):
+        whole = prod.at[d]
+
+        @when(d > p)
+        def _():
+            send(whole, rin.at[d], rs.at[d], rr.at[d, 0], me).wait_send()
+
+        @when(d < p)
+        def _():
+            send(whole, lin.at[d], ls.at[d], lr.at[d, 0], me).wait_send()
+
+    loop(zl, drain)
+
+    def drain_scan(g):
+        all_of(g, a_s, a_r, lanes - 1).wait_send()
+        all_of(g, b_s, b_r, lanes - 1).wait_send()
+        for q in range(NY - 1):
+
+            @when(y == q)
+            def _(q=q):
+                all_of(g, y_s, y_r, NY - 1 - q).wait_send()
 
         z_copy(g).wait_send()
-        return 0
-
-    lax.fori_loop(0, groups, drain_scan, 0)
+
+    loop(groups, drain_scan)
 
 
 def local(zl, tap_matrices, density_history, offsets, column_slots):
@@ -361,13 +377,13 @@
             dma((1,)), dma((1,)),
             dma((NX,)), dma((1,)),
             dma((1,)), dma((NX,)),
-            pltpu.SemaphoreType.REGULAR,
-            dma((zl, groups)), dma((zl, groups)),
-            dma((zl, groups)), dma((zl, groups)),
-            dma((groups, lanes)), dma((groups, lanes)),
-            dma((groups, NY)), dma((groups, NY)),
+            pltpu.SemaphoreType.REGULAR((2,)),
+            dma((zl,)), dma((zl, groups)),
+            dma((zl,)), dma((zl, groups)),
             dma((groups,)), dma((groups,)),
-            dma((groups, lanes)), dma((groups, lanes)),
+            dma((groups,)), dma((groups,)),
+            dma((groups,)), dma((groups,)),
+            dma((groups,)), dma((groups,)),
         ],
         compiler_params=pltpu.CompilerParams(collective_id=0, has_side_effects=True, vmem_limit_bytes=62 << 20),
     )(offsets, column_slots, tap_matrices.reshape(m, c), density_history)

time: 78.5 us -> 75 us (0.955)
  Pallas kernels: 75.8 us -> 72.5 us
    pallas_call x1, Pallas kernels: 75.8 us -> 72.5 us  [local(): pl.pallas_call(functools.partial(kernel, zl), out_shape=jax.ShapeDtypeStr...]
where the time goes in v3:
time: 75 us; the launch traced here: 74.7 us
  Pallas kernels  72.5 us (97%)
  local copies, waits for them, and re-layouts  1.62 us (2%)
    pallas_call x1, Pallas kernels, local(): pl.pallas_call(functools.partial(kernel, zl), out_shape=jax.ShapeDtypeStr...  72.5 us
    unnamed x1, local copies, waits for them, and re-layouts  1.62 us

profile of v3, /device:TPU:25, one launch (start us, length us, event | category | flops | bytes accessed | tf_op | source)
XLA Modules:
  0.0 74.7 jit_solution(14931332164360133392)
XLA Ops:
  0.7 72.5 %shard_map.46 = f32[3,128,128]{2,1,0:T(8,128)} custom-call(s32[1]{0:T(128)S(6)} %copy.6.off_ref, s32[1,128]{1,0:T(1,128)} %slots_hbm.1, bf16[1024,1024]{1,0:T(8,128)(2,1)} %bitcast.4, bf16[4,1024,128]{2,1,0:T(8,128)(2,1)} %dens_hbm.1), custom_call_target="tpu_custom_call" | custom-call | tf_op jit(solution)/shard_map/pallas_call | solution.py:348
  73.1 1.6 %copy.7 = f32[1,128,3,128]{3,1,2,0:T(8,128)} copy(f32[1,128,3,128]{3,1,2,0:T(8,128)} %bitcast.5) | data formatting | bytes 393216

commit v4 on v3

--- a/solution.py
+++ b/solution.py
@@ -16,7 +16,7 @@
 D2, D3, D4, D5 = 7, 14, 29, 36
 
 
-def kernel(zl, off_ref, slots_hbm, tap_hbm, dens_hbm, out_ref, slots_ref, tap, win, dmat, prod, rin, lin, gath, pre, tot, yin, exb, zout, zin,
+def kernel(zl, off_ref, slots_hbm, tap_hbm, dens_hbm, out_ref, slots_ref, tap, win, dmat, prod, sent, sent_low, rin, rin_low, lin, lin_low, token, gath, pre, tot, yin, exb, zout, zin,
            fin, res, rela, loc, nb_s, nb_r, ca_s, ca_r, cb_s, cb_r, hello, rs, rr, ls, lr, a_s, a_r, y_s, y_r, z_s, z_r,
            b_s, b_r):
     lag, p = lax.axis_index("lag"), lax.axis_index("col")
@@ -180,14 +180,38 @@
     def _():
         vouch()
 
-    def move(step, hops, sign, buf, ssem, rsem):
-        def copy(d, g, to):
-            return send(prod.at[d, g], buf.at[d, g], ssem.at[d], rsem.at[d, g], to)
+    half = rows // 2
+
+    def pack(value, d, g):
+        high = value.astype(jnp.bfloat16)
+        wide = high.astype(jnp.float32)
+        share = (value - wide) / jnp.where(wide == 0.0, 1.0, wide) * 32768.0
+        steps = (jnp.clip(share, -127.0, 127.0) + 128.5).astype(jnp.int32) - 128
+        sent[d, g] = high
+        sent_low[d, g] = (steps[:half] + steps[half:] * 256).astype(jnp.int16)
+
+    def unpacked(high, low):
+        both = low.astype(jnp.int32)
+        upper = ((both + 128) & 255) - 128
+        lower = (both - upper) >> 8
+        wide = high.astype(jnp.float32)
+        steps = jnp.concatenate([upper, lower], axis=0).astype(jnp.float32)
+        return wide + wide * (steps * (1.0 / 32768.0))
+
+    def move(step, hops, sign, buf, buf_low, ssem, rsem):
+        def pass_on(d, g):
+            send(sent.at[d, g], buf.at[d, g], ssem.at[d], rsem.at[d, g], (lag, p + sign)).start()
+            send(sent_low.at[d, g], buf_low.at[d, g], ssem.at[d], rsem.at[d, g], (lag, p + sign)).start()
 
         @when((hops == 0) & (step < last))
         def _():
             d = last - step if sign > 0 else step
-            loop(groups, lambda g: copy(d, g, (lag, p + sign)).start())
+
+            def one_piece(g):
+                pack(prod[d, g], d, g)
+                pass_on(d, g)
+
+            loop(groups, one_piece)
 
         n = step - HOP * hops
 
@@ -196,12 +220,18 @@
             i = n // groups
             g = n % groups
             d = last - i if sign > 0 else i
-            copy(d, g, me).wait_recv()
-            prod[d, g] = prod[d, g] + buf[d, g]
+            both = token.at[pl.ds(0, rows + half)]
+            send(both, both, ssem.at[d], rsem.at[d, g], me).wait_recv()
+            value = prod[d, g] + unpacked(buf[d, g], buf_low[d, g])
+
+            @when(d == p)
+            def _():
+                prod[d, g] = value
 
             @when(d != p)
             def _():
-                copy(d, g, (lag, p + sign)).start()
+                pack(value, d, g)
+                pass_on(d, g)
 
     def mine(j):
         return pl.ds(pl.multiple_of(j * piece, piece), piece)
@@ -284,8 +314,8 @@
         def _():
             loop(2, lambda k: product(2 * s + k))
 
-        move(s, p, 1, rin, rs, rr)
-        move(s, last - p, -1, lin, ls, lr)
+        move(s, p, 1, rin, rin_low, rs, rr)
+        move(s, last - p, -1, lin, lin_low, ls, lr)
 
         for delay, stage in ((0, stage1), (D2, stage2), (D3, stage3), (D4, stage4), (D5, stage5)):
             g = s - base - delay
@@ -312,15 +342,13 @@
         leg_b().wait_send()
 
     def drain(d):
-        whole = prod.at[d]
-
         @when(d > p)
         def _():
-            send(whole, rin.at[d], rs.at[d], rr.at[d, 0], me).wait_send()
+            send(token, token, rs.at[d], rr.at[d, 0], me).wait_send()
 
         @when(d < p)
         def _():
-            send(whole, lin.at[d], ls.at[d], lr.at[d, 0], me).wait_send()
+            send(token, token, ls.at[d], lr.at[d, 0], me).wait_send()
 
     loop(zl, drain)
 
@@ -361,8 +389,10 @@
             vmem((6, c, E), bf16),
             vmem((c, TICKS * E), bf16),
             vmem((zl, groups, rows, E), f32),
-            vmem((zl, groups, rows, E), f32),
-            vmem((zl, groups, rows, E), f32),
+            vmem((zl, groups, rows, E), bf16), vmem((zl, groups, rows // 2, E), jnp.int16),
+            vmem((zl, groups, rows, E), bf16), vmem((zl, groups, rows // 2, E), jnp.int16),
+            vmem((zl, groups, rows, E), bf16), vmem((zl, groups, rows // 2, E), jnp.int16),
+            vmem((groups * (rows + rows // 2), E), bf16),
             vmem((groups, lanes, piece, E), f32),
             vmem((groups, lanes, piece, E), f32),
             vmem((groups, piece, E), f32),

time: 75 us -> 71.7 us (0.956)
  Pallas kernels: 72.5 us -> 69.3 us
    pallas_call x1, Pallas kernels: 72.5 us -> 69.3 us  [local(): pl.pallas_call(functools.partial(kernel, zl), out_shape=jax.ShapeDtypeStr...]
where the time goes in v4:
time: 71.7 us; the launch traced here: 71.6 us
  Pallas kernels  69.3 us (97%)
  local copies, waits for them, and re-layouts  1.62 us (2%)
    pallas_call x1, Pallas kernels, local(): pl.pallas_call(functools.partial(kernel, zl), out_shape=jax.ShapeDtypeStr...  69.3 us
    unnamed x1, local copies, waits for them, and re-layouts  1.62 us

profile of v4, /device:TPU:25, one launch (start us, length us, event | category | flops | bytes accessed | tf_op | source)
XLA Modules:
  0.0 71.6 jit_solution(6928921753627797327)
XLA Ops:
  0.7 69.3 %shard_map.46 = f32[3,128,128]{2,1,0:T(8,128)} custom-call(s32[1]{0:T(128)S(6)} %copy.6.off_ref, s32[1,128]{1,0:T(1,128)} %slots_hbm.1, bf16[1024,1024]{1,0:T(8,128)(2,1)} %bitcast.4, bf16[4,1024,128]{2,1,0:T(8,128)(2,1)} %dens_hbm.1), custom_call_target="tpu_custom_call" | custom-call | tf_op jit(solution)/shard_map/pallas_call | solution.py:376
  70.0 1.6 %copy.7 = f32[1,128,3,128]{3,1,2,0:T(8,128)} copy(f32[1,128,3,128]{3,1,2,0:T(8,128)} %bitcast.5) | data formatting | bytes 393216

commit v5 on v4

--- a/solution.py
+++ b/solution.py
@@ -12,7 +12,8 @@
 TICKS = 3
 E = 128
 HALVES = 2
-HOP = 6
+HOP, LATE_HOP = 8, 7
+CUTS = 2
 D2, D3, D4, D5 = 7, 14, 29, 36
 
 
@@ -97,13 +98,11 @@
 
     @when(cross_dst & jnp.logical_not(final))
     def _():
-        zh_, p_ = round_z(z - eighth)
         for j in range(NX):
-            greet(at(y + zh, zh_, j, 1, p_))
+            greet(at(y + zh, 1 - zh, j, 1, p))
 
     one = lambda c: c.astype(jnp.int32)
-    far = round_z(z + eighth)[0]
-    many = lanes - 1 + one(p > 0) + one(p < last) + NY - 1 - y + 2 + one((core == 1) & ((y > 0) | (far == 0)))
+    many = lanes - 1 + one(p > 0) + one(p < last) + NY - 1 - y + 2 + one(has_a)
     pl.semaphore_wait(barrier, many)
     for dz in (eighth, -eighth):
         pl.semaphore_signal(hello.at[0], inc=1, device_id=along(dz), device_id_type=MESH)
@@ -122,44 +121,44 @@
     def _():
         neighbour().start()
 
-    def part_of(ref, j, first):
-        return ref.at[first + j // (NX // 2), pl.ds((j % (NX // 2)) * part, part)]
-
-    def leg_a(j):
-        return send(part_of(dens_hbm, j, 0), rela, ca_s.at[j], ca_r.at[0], at(y, zh, j, 1, p))
-
-    def leg_b():
-        return send(rela, part_of(win, x, 4), cb_s.at[0], cb_r.at[x], at(y - (1 - zh), 1 - zh, NX - 1, 1, p))
+    piece_of = part // CUTS
+
+    def part_of(ref, j, first, i=0, size=part):
+        return ref.at[first + j // (NX // 2), pl.ds((j % (NX // 2)) * part + i * piece_of, size)]
+
+    def leg_a(j, i):
+        return send(part_of(dens_hbm, j, 0, i, piece_of), rela.at[i], ca_s.at[j], ca_r.at[i], at(y, zh, j, 1, p))
+
+    def leg_b(i):
+        there = at(y - (1 - zh), 1 - zh, NX - 1, 1, p)
+        return send(rela.at[i], part_of(win, x, 4, i, piece_of), cb_s.at[i], cb_r.at[x], there)
 
     @when(sends_a)
     def _():
+        for i in range(CUTS):
+            for j in range(NX):
+                leg_a(j, i).start()
+
+    @when(has_a)
+    def _():
+        for i in range(CUTS):
+            leg_a(0, i).wait_recv()
+            leg_b(i).start()
+
+    @when(final)
+    def _():
+        win[pl.ds(4, 2)] = jnp.zeros((2, *win.shape[1:]), win.dtype)
+
+    get_dens.wait()
+
+    @when(jnp.logical_not(cross_dst))
+    def _():
+        neighbour().wait_recv()
+
+    @when(cross_dst & jnp.logical_not(final))
+    def _():
         for j in range(NX):
-            leg_a(j).start()
-
-    @when(core == 1)
-    def _():
-        vouch()
-        vouched()
-
-    @when(has_a)
-    def _():
-        leg_a(0).wait_recv()
-        leg_b().start()
-
-    @when(final)
-    def _():
-        win[pl.ds(4, 2)] = jnp.zeros((2, *win.shape[1:]), win.dtype)
-
-    get_dens.wait()
-
-    @when(jnp.logical_not(cross_dst))
-    def _():
-        neighbour().wait_recv()
-
-    @when(cross_dst & jnp.logical_not(final))
-    def _():
-        for j in range(NX):
-            send(rela, part_of(win, j, 4), cb_s.at[0], cb_r.at[j], me).wait_recv()
+            send(part_of(win, j, 4), part_of(win, j, 4), cb_s.at[0], cb_r.at[j], me).wait_recv()
 
     get_slots.wait()
     perm = (lax.broadcasted_iota(jnp.int32, (E, E), 0) == slots_ref[...]).astype(jnp.float32).astype(jnp.bfloat16)
@@ -176,11 +175,10 @@
             for h in range(HALVES):
                 prod[d, t * HALVES + h] = block[h * rows : (h + 1) * rows, t * E : (t + 1) * E]
 
-    @when(core == 0)
-    def _():
-        vouch()
+    vouch()
 
     half = rows // 2
+    hop = jnp.where(cross_dst, LATE_HOP, HOP)
 
     def pack(value, d, g):
         high = value.astype(jnp.bfloat16)
@@ -213,7 +211,7 @@
 
             loop(groups, one_piece)
 
-        n = step - HOP * hops
+        n = step - hop * hops
 
         @when((hops > 0) & (n >= 0) & (n < (zl - hops) * groups))
         def _():
@@ -282,7 +280,7 @@
 
         loop(y, add)
 
-        @when((core == 0) & (g == 0))
+        @when(g == 0)
         def _():
             vouched()
 
@@ -302,12 +300,13 @@
         out_ref[g // HALVES, pl.ds(pl.multiple_of((g % HALVES) * rows, rows), rows)] = res[g]
 
     def ready(q):
-        right = jnp.where(q > 0, HOP * q + (last - q) * groups, 0)
-        left = jnp.where(q < last, HOP * (last - q) + q * groups, 0)
+        right = jnp.where(q > 0, hop * q + (last - q) * groups, 0)
+        left = jnp.where(q < last, hop * (last - q) + q * groups, 0)
         return jnp.maximum(right, left)
 
     base = ready(p)
-    longest = max(max(HOP * q + (last - q) * groups if q else 0, HOP * (last - q) + q * groups if q < last else 0) for q in range(zl))
+    most = max(HOP, LATE_HOP)
+    longest = max(most * q + max(last - q, 0) * groups for q in range(zl))
 
     def step(s, _):
         @when(s < zl // 2)
@@ -335,11 +334,12 @@
     @when(sends_a)
     def _():
         for j in range(NX):
-            leg_a(j).wait_send()
+            send(part_of(dens_hbm, j, 0), part_of(win, j, 4), ca_s.at[j], ca_r.at[0], me).wait_send()
 
     @when(has_a)
     def _():
-        leg_b().wait_send()
+        for i in range(CUTS):
+            leg_b(i).wait_send()
 
     def drain(d):
         @when(d > p)
@@ -402,11 +402,11 @@
             vmem((groups, piece, E), f32),
             vmem((groups, lanes, piece, E), f32),
             vmem((groups, rows, E), f32),
-            vmem((part, E), bf16),
+            vmem((CUTS, part // CUTS, E), bf16),
             dma((3,)),
             dma((1,)), dma((1,)),
-            dma((NX,)), dma((1,)),
-            dma((1,)), dma((NX,)),
+            dma((NX,)), dma((CUTS,)),
+            dma((CUTS,)), dma((NX,)),
             pltpu.SemaphoreType.REGULAR((2,)),
             dma((zl,)), dma((zl, groups)),
             dma((zl,)), dma((zl, groups)),

time: 71.7 us -> 70.7 us (0.986)
  Pallas kernels: 69.3 us -> 68.3 us
    pallas_call x1, Pallas kernels: 69.3 us -> 68.3 us  [local(): pl.pallas_call(functools.partial(kernel, zl), out_shape=jax.ShapeDtypeStr...]
where the time goes in v5:
time: 70.7 us; the launch traced here: 70.6 us
  Pallas kernels  68.3 us (97%)
  local copies, waits for them, and re-layouts  1.62 us (2%)
    pallas_call x1, Pallas kernels, local(): pl.pallas_call(functools.partial(kernel, zl), out_shape=jax.ShapeDtypeStr...  68.3 us
    unnamed x1, local copies, waits for them, and re-layouts  1.62 us

profile of v5, /device:TPU:25, one launch (start us, length us, event | category | flops | bytes accessed | tf_op | source)
XLA Modules:
  0.0 70.6 jit_solution(4846940571464802031)
XLA Ops:
  0.7 68.3 %shard_map.46 = f32[3,128,128]{2,1,0:T(8,128)} custom-call(s32[1]{0:T(128)S(6)} %copy.6.off_ref, s32[1,128]{1,0:T(1,128)} %slots_hbm.1, bf16[1024,1024]{1,0:T(8,128)(2,1)} %bitcast.4, bf16[4,1024,128]{2,1,0:T(8,128)(2,1)} %dens_hbm.1), custom_call_target="tpu_custom_call" | custom-call | tf_op jit(solution)/shard_map/pallas_call | solution.py:376
  69.0 1.6 %copy.7 = f32[1,128,3,128]{3,1,2,0:T(8,128)} copy(f32[1,128,3,128]{3,1,2,0:T(8,128)} %bitcast.5) | data formatting | bytes 393216

commit v6 on v5

--- a/solution.py
+++ b/solution.py
@@ -13,6 +13,7 @@
 E = 128
 HALVES = 2
 HOP, LATE_HOP = 8, 7
+VOUCH = 7
 CUTS = 2
 D2, D3, D4, D5 = 7, 14, 29, 36
 
@@ -175,7 +176,6 @@
             for h in range(HALVES):
                 prod[d, t * HALVES + h] = block[h * rows : (h + 1) * rows, t * E : (t + 1) * E]
 
-    vouch()
 
     half = rows // 2
     hop = jnp.where(cross_dst, LATE_HOP, HOP)
@@ -313,6 +313,7 @@
         def _():
             loop(2, lambda k: product(2 * s + k))
 
+        pl.when(s == VOUCH)(vouch)
         move(s, p, 1, rin, rin_low, rs, rr)
         move(s, last - p, -1, lin, lin_low, ls, lr)
 

time: 70.7 us -> 70.3 us (level)
  no operation moved by 1% of the time
where the time goes in v6:
time: 70.3 us; the launch traced here: 70.2 us
  Pallas kernels  67.9 us (97%)
  local copies, waits for them, and re-layouts  1.62 us (2%)
    pallas_call x1, Pallas kernels, local(): pl.pallas_call(functools.partial(kernel, zl), out_shape=jax.ShapeDtypeStr...  67.9 us
    unnamed x1, local copies, waits for them, and re-layouts  1.62 us

profile of v6, /device:TPU:25, one launch (start us, length us, event | category | flops | bytes accessed | tf_op | source)
XLA Modules:
  0.0 70.2 jit_solution(8300514789637452)
XLA Ops:
  0.7 67.9 %shard_map.46 = f32[3,128,128]{2,1,0:T(8,128)} custom-call(s32[1]{0:T(128)S(6)} %copy.6.off_ref, s32[1,128]{1,0:T(1,128)} %slots_hbm.1, bf16[1024,1024]{1,0:T(8,128)(2,1)} %bitcast.4, bf16[4,1024,128]{2,1,0:T(8,128)(2,1)} %dens_hbm.1), custom_call_target="tpu_custom_call" | custom-call | tf_op jit(solution)/shard_map/pallas_call | solution.py:377
  68.5 1.6 %copy.7 = f32[1,128,3,128]{3,1,2,0:T(8,128)} copy(f32[1,128,3,128]{3,1,2,0:T(8,128)} %bitcast.5) | data formatting | bytes 393216
